TPU v7x, 512 devices: a whole 4x8x8 slice. The times are simulated.
512 devices in a mesh: expert: 8 (over x, core), tensor: 64 (over y, z).
Axes of the slice: x: 4, y: 8, z: 8, core: 2. Of those that a mesh axis runs over, the one named last changes fastest.
Arguments:
- tokens: bfloat16 [1536, 6144], P('tensor'), may hold values from -6 to 6
- expert_ids: int32 [1536, 2], P('tensor'), may hold values from 0 to 7, all different within a row; in each aligned block of 24 rows (0 to 23, 24 to 47, ...) at most 12 rows name the same one
- gate_units: int32 [1536, 2], P('tensor'), may hold values from 1 to 65535
- gate_weight: bfloat16 [8, 6144, 8192], P('expert', None, 'tensor'), may hold values from -0.078125 to 0.078125
- up_weight: bfloat16 [8, 6144, 8192], P('expert', None, 'tensor'), may hold values from -0.078125 to 0.078125
- down_weight: bfloat16 [8, 6144, 8192], P('expert', 'tensor'), may hold values from -0.0625 to 0.0625
Outputs:
- expert_mix: bfloat16 [1536, 6144], P('tensor', 'expert')
Inputs may be any that keep to these rules, and one draw needn't show every extreme that they name: `expert_ids`: within each aligned block of 24 rows (the tokens of one tensor index) the two ids of a row differ and no expert is named by more than 12 rows; in every draw some expert is named by exactly 12 rows of some block, and every expert is named somewhere.
All inputs are finite; a program needn't handle non-finite values.
Results may differ from a plain program's by a relative error of at most 0.0057.
Values may be sent and summed in bfloat16 or wider, within the bound.
A program may use at most 128 MiB of HBM per device.

v0:
```python
import jax
import jax.numpy as jnp
from jax import lax
from jax.sharding import PartitionSpec as P


def slot_tables(expert_ids, gate_units, expert_id, capacity):
    tok_rows = expert_ids.shape[0]
    top_count = expert_ids.shape[1]
    flat_route = expert_ids.reshape(-1)
    matches = (flat_route == expert_id).astype(jnp.int32)
    slot_rank = jnp.cumsum(matches) - matches
    slot_ids = jnp.arange(capacity, dtype=jnp.int32)
    assignment = jnp.where(
        (slot_rank[None, :] == slot_ids[:, None]) & (matches[None, :] == 1), 1.0, 0.0
    ).astype(jnp.float32)
    positions = jnp.arange(tok_rows * top_count, dtype=jnp.int32) // top_count
    owners = (positions[:, None] == jnp.arange(tok_rows, dtype=jnp.int32)[None, :]).astype(
        jnp.float32
    )
    unit_vals = gate_units.astype(jnp.float32)
    shares = unit_vals / jnp.sum(unit_vals, axis=1, keepdims=True)
    picker = jnp.dot(
        assignment, owners, precision=lax.Precision.HIGHEST, preferred_element_type=jnp.float32
    )
    weighted = jnp.dot(
        assignment,
        owners * shares.reshape(-1)[:, None],
        precision=lax.Precision.HIGHEST,
        preferred_element_type=jnp.float32,
    )
    return (picker, weighted)


def local(tokens, expert_ids, gate_units, gate_weight, up_weight, down_weight):
    experts = lax.axis_size("expert")
    expert_id = lax.axis_index("expert")
    tok_rows = tokens.shape[0]
    capacity = min(tok_rows, 4 * tok_rows // experts)
    picker, weighted = slot_tables(expert_ids, gate_units, expert_id, capacity)
    picked = jnp.dot(
        picker.astype(jnp.bfloat16), tokens, preferred_element_type=jnp.float32
    ).astype(jnp.bfloat16)
    w_gate = gate_weight[0]
    w_up = up_weight[0]
    w_down = down_weight[0]
    shard_piece = lax.all_gather(picked, "tensor", axis=0, tiled=True)
    gate_vals = jnp.dot(shard_piece, w_gate, preferred_element_type=jnp.float32)
    up_vals = jnp.dot(shard_piece, w_up, preferred_element_type=jnp.float32)
    hidden = (jax.nn.silu(gate_vals) * up_vals).astype(jnp.bfloat16)
    gathered = lax.all_gather(hidden, "tensor", axis=1, tiled=True)
    projected = lax.dot_general(
        gathered, w_down, (((1,), (1,)), ((), ())), preferred_element_type=jnp.float32
    )
    outputs = projected.astype(jnp.bfloat16)
    returned = lax.all_to_all(outputs, "tensor", split_axis=0, concat_axis=1, tiled=True)
    contribution = lax.dot_general(
        weighted,
        returned.astype(jnp.float32),
        (((0,), (0,)), ((), ())),
        precision=lax.Precision.HIGHEST,
        preferred_element_type=jnp.float32,
    )
    summed_all = lax.psum(contribution, "expert")
    col_width = contribution.shape[1] // experts
    mixed = lax.dynamic_slice_in_dim(summed_all, expert_id * col_width, col_width, 1)
    return mixed.astype(jnp.bfloat16)


def solution(mesh):
    return jax.shard_map(
        local,
        mesh=mesh,
        in_specs=(
            P("tensor", None),
            P("tensor", None),
            P("tensor", None),
            P("expert", None, "tensor"),
            P("expert", None, "tensor"),
            P("expert", "tensor", None),
        ),
        out_specs=P("tensor", "expert"),
        check_vma=False,
    )
```

profile of v0, /device:TPU:8, one launch (start us, length us, event | category | flops | bytes accessed | tf_op | source)
XLA Modules:
  0.0 349.5 jit_solution(7697855502720402069)
XLA Ops:
  6.5 0.0 copy-start
  6.5 0.0 all-gather.6.cloned.1.call-start
  6.5 0.8 compare_convert_fusion
  7.3 0.1 copy.17
  7.4 0.1 reshape.76
  7.5 0.1 reshape.79
  7.6 0.1 reduce-window.8
  7.7 0.1 reduce
  7.8 0.2 convolution_convert_fusion.1
  8.0 1.8 fusion
  9.9 0.0 all-gather.6.cloned.1.call-update
  9.9 0.0 all-gather.4.cloned.1.call-start
  9.9 124.4 %all-gather.6.cloned.1.call-done = bf16[64,12,6144]{2,1,0:T(8,128)(2,1)} async-done(((bf16[1,12,6144]{2,1,0:T(8,128)(2,1)}), bf16[64,12,6144]{2,1,0:T(8,128)(2,1)}) %all-gather.6.cloned.1.call-update) | async-done | bytes 9437200 | tf_op jit(solution)/shard_map/all_gather | solution.py:47
  134.3 13.7 %reshape.78 = bf16[768,6144]{1,0:T(8,128)(2,1)} reshape(bf16[64,12,6144]{2,1,0:T(8,128)(2,1)} %all-gather.6.cloned.1.call-done) | data formatting | bytes 18874368
  148.1 0.0 copy-done
  148.1 0.0 copy-start.1
  148.1 0.0 copy-start.4
  148.1 6.1 %fusion.5 = f32[768,128]{1,0:T(8,128)S(1)} fusion(bf16[768,6144]{1,0:T(8,128)(2,1)} %reshape.78, bf16[1,6144,128]{2,1,0:T(8,128)(2,1)S(1)} %copy-done), kind=kOutput, calls=%fused_computation.6 | convolution fusion | flops 1207959552 | bytes 11403264 | tf_op jit(solution)/shard_map/dot_general | solution.py:48
  154.2 0.3 copy-done.1
  154.5 0.4 copy-done.4
  154.9 0.0 copy-start.3
  154.9 0.0 copy-start.2
  155.0 3.3 fusion.10
  158.2 0.0 all-gather.4.cloned.1.call-update
  158.2 0.0 copy-done.3
  158.3 124.2 %all-gather.4.cloned.1.call-done = bf16[768,8192]{1,0:T(8,128)(2,1)} async-done(((bf16[768,128]{1,0:T(8,128)(2,1)}), bf16[768,8192]{1,0:T(8,128)(2,1)}) %all-gather.4.cloned.1.call-update) | async-done | bytes 12582928 | tf_op jit(solution)/shard_map/all_gather | solution.py:51
  282.5 0.0 copy-done.2
  282.5 8.6 %fusion.13 = bf16[768,96]{0,1:T(8,128)(2,1)S(1)} fusion(bf16[768,8192]{1,0:T(8,128)(2,1)} %all-gather.4.cloned.1.call-done, bf16[1,96,8192]{2,1,0:T(8,128)(2,1)S(1)} %copy-done.2), kind=kOutput, calls=%fused_computation.10 | convolution fusion | flops 1208033280 | bytes 14303232 | tf_op jit(solution)/shard_map/dot_general | solution.py:52
  291.1 0.2 copy.21
  291.3 0.8 all_to_all.14
  292.0 7.8 %all-to-all-start = ((bf16[64,12,96]{2,1,0:T(8,128)(2,1)}), bf16[64,12,96]{2,1,0:T(8,128)(2,1)S(1)}, u32[]{:S(2)}, u32[]{:S(2)}) async-start(bf16[64,12,96]{2,1,0:T(8,128)(2,1)} %all_to_all.14), calls=%async_computation | async-start | bytes 524288 | tf_op jit(solution)/shard_map/all_to_all | solution.py:56
  299.8 0.1 copy.20
  299.9 0.1 mul.20
  300.0 0.2 fusion.16
  300.2 12.0 %all-to-all-done = bf16[64,12,96]{2,1,0:T(8,128)(2,1)S(1)} async-done(((bf16[64,12,96]{2,1,0:T(8,128)(2,1)}), bf16[64,12,96]{2,1,0:T(8,128)(2,1)S(1)}, u32[]{:S(2)}, u32[]{:S(2)}) %all-to-all-start) | async-done | bytes 147488 | tf_op jit(solution)/shard_map/all_to_all | solution.py:56
  312.2 0.1 copy.22
  312.2 0.3 all_to_all.17
  312.5 0.4 fusion.39
  313.0 29.1 %all-reduce.1 = bf16[24,6144]{1,0:T(8,128)(2,1)S(1)} all-reduce(f32[24,6144]{1,0:T(8,128)S(1)} %fusion.39), channel_id=1, replica_groups=mesh['expert'=8,'tensor'=64] {'expert'}, use_global_device_ids=true, to_apply=%region_2.3 | all-reduce | flops 147456 | bytes 884736 | tf_op jit(solution)/shard_map/psum | solution.py:64
  342.0 0.6 dynamic-slice_convert_fusion
  (5 shorter events, 0.0 us)
Async XLA Ops:
  6.5 141.6 %copy-start = (bf16[1,6144,128]{2,1,0:T(8,128)(2,1)S(1)}, bf16[1,6144,128]{2,1,0:T(8,128)(2,1)}, u32[]{:S(2)}) copy-start(bf16[1,6144,128]{2,1,0:T(8,128)(2,1)} %param.9) | copy-start | bytes 4718596
  6.5 127.8 %all-gather.6.cloned.1.call-start = ((), (), s32[]{:S(2)}) async-start(), calls=%async_computation.2 | async-start | bytes 12779520 | tf_op jit(solution)/shard_map/all_gather | solution.py:47
  9.9 272.6 %all-gather.4.cloned.1.call-start = ((), (), s32[]{:S(2)}) async-start(), calls=%async_computation.1 | async-start | bytes 12779520 | tf_op jit(solution)/shard_map/all_gather | solution.py:51
  148.1 6.4 %copy-start.1 = (bf16[768,6144]{1,0:T(8,128)(2,1)S(1)}, bf16[768,6144]{1,0:T(8,128)(2,1)}, u32[]{:S(2)}) copy-start(bf16[768,6144]{1,0:T(8,128)(2,1)} %reshape.78) | copy-start | bytes 28311556
  148.1 6.9 %copy-start.4 = (bf16[1,6144,128]{2,1,0:T(8,128)(2,1)S(1)}, bf16[1,6144,128]{2,1,0:T(8,128)(2,1)}, u32[]{:S(2)}) copy-start(bf16[1,6144,128]{2,1,0:T(8,128)(2,1)} %param.10) | copy-start | bytes 4718596
  154.9 3.3 copy-start.3
  154.9 127.6 %copy-start.2 = (bf16[1,96,8192]{2,1,0:T(8,128)(2,1)S(1)}, bf16[1,96,8192]{2,1,0:T(8,128)(2,1)}, u32[]{:S(2)}) copy-start(bf16[1,96,8192]{2,1,0:T(8,128)(2,1)} %param.11) | copy-start | bytes 4718596
  292.0 20.1 %all-to-all-start = ((bf16[64,12,96]{2,1,0:T(8,128)(2,1)}), bf16[64,12,96]{2,1,0:T(8,128)(2,1)S(1)}, u32[]{:S(2)}, u32[]{:S(2)}) async-start(bf16[64,12,96]{2,1,0:T(8,128)(2,1)} %all_to_all.14), calls=%async_computation | async-start | bytes 524288 | tf_op jit(solution)/shard_map/all_to_all | solution.py:56
Sparse Core Ops, SparseCore 0:
  10.4 123.9 all-gather.5
  158.4 124.1 all-gather.3
where the time goes:
time: 350 us
  waiting for transfers between devices  261 us (75%)
  blocking collectives  29.1 us (8%)
  matrix products  20.7 us (6%)
  local copies, waits for them, and re-layouts  16.8 us (5%)
  between operations  13.5 us (4%)
  starting transfers between devices  7.81 us (2%)
    all_gather x1, waiting for transfers between devices, local(): shard_piece = lax.all_gather(picked, 'tensor', axis=0, tiled=True)  124 us
    all_gather x1, waiting for transfers between devices, local(): gathered = lax.all_gather(hidden, 'tensor', axis=1, tiled=True)  124 us
    psum x1, blocking collectives, local(): summed_all = lax.psum(contribution, 'expert')  29.1 us
    unnamed x11, local copies, waits for them, and re-layouts  14.5 us
    all_to_all x1, waiting for transfers between devices, local(): lax.all_to_all(outputs, 'tensor', split_axis=0, concat_axis=1, tiled=True)  12 us
    dot_general x1, matrix products, local(): lax.dot_general(gathered, w_down, (((1,), (1,)), ((), ())), preferred_ele...  8.57 us
    all_to_all x1, starting transfers between devices, local(): lax.all_to_all(outputs, 'tensor', split_axis=0, concat_axis=1, tiled=True)  7.77 us
  transfers between devices with their start and end apart: 3, of which 3 were waited for; matrix products, arithmetic and copies ran while one was open for 0% of the time, Pallas kernels for 0%

commit v1 on v0

--- a/solution.py
+++ b/solution.py
@@ -61,7 +61,10 @@
         precision=lax.Precision.HIGHEST,
         preferred_element_type=jnp.float32,
     )
-    summed_all = lax.psum(contribution, "expert")
+    size, summed_all = (lax.axis_size("expert"), contribution)
+    for hop in [1 << k for k in range(size.bit_length() - 1)]:
+        route = [(i, i ^ hop) for i in range(size)]
+        summed_all = summed_all + lax.ppermute(summed_all, "expert", route)
     col_width = contribution.shape[1] // experts
     mixed = lax.dynamic_slice_in_dim(summed_all, expert_id * col_width, col_width, 1)
     return mixed.astype(jnp.bfloat16)

time: 350 us -> 362 us (1.034)
  the two profiles are of different devices: /device:TPU:8 before, /device:TPU:2 now
where the time goes in v1:
time: 362 us; the launch traced here: 361 us
  waiting for transfers between devices  293 us (81%)
  matrix products  20.6 us (6%)
  local copies, waits for them, and re-layouts  16.2 us (4%)
  starting transfers between devices  15.9 us (4%)
  between operations  13.5 us (4%)
    all_gather x1, waiting for transfers between devices, local(): shard_piece = lax.all_gather(picked, 'tensor', axis=0, tiled=True)  124 us
    all_gather x1, waiting for transfers between devices, local(): gathered = lax.all_gather(hidden, 'tensor', axis=1, tiled=True)  124 us
    ppermute x3, waiting for transfers between devices, local(): summed_all = summed_all + lax.ppermute(summed_all, 'expert', route)  30.9 us
    unnamed x11, local copies, waits for them, and re-layouts  14.5 us
    all_to_all x1, waiting for transfers between devices, local(): lax.all_to_all(outputs, 'tensor', split_axis=0, concat_axis=1, tiled=True)  13.3 us
    dot_general x1, matrix products, local(): lax.dot_general(gathered, w_down, (((1,), (1,)), ((), ())), preferred_ele...  8.57 us
    ppermute x3, starting transfers between devices, local(): summed_all = summed_all + lax.ppermute(summed_all, 'expert', route)  8.18 us
    all_to_all x1, starting transfers between devices, local(): lax.all_to_all(outputs, 'tensor', split_axis=0, concat_axis=1, tiled=True)  7.64 us
  transfers between devices with their start and end apart: 6, of which 6 were waited for; matrix products, arithmetic and copies ran while one was open for 0% of the time, Pallas kernels for 0%

profile of v1, /device:TPU:2, one launch (start us, length us, event | category | flops | bytes accessed | tf_op | source)
XLA Modules:
  0.0 360.9 jit_solution(2555757021935219371)
XLA Ops:
  6.5 0.0 copy-start
  6.5 0.0 all-gather.6.cloned.1.call-start
  6.5 0.8 compare_convert_fusion
  7.3 0.1 copy.17
  7.4 0.1 reshape.76
  7.5 0.1 reshape.79
  7.6 0.1 reduce-window.8
  7.7 0.1 reduce
  7.8 0.2 convolution_convert_fusion.1
  8.0 1.8 fusion
  9.9 0.0 all-gather.6.cloned.1.call-update
  9.9 0.0 all-gather.4.cloned.1.call-start
  9.9 124.5 %all-gather.6.cloned.1.call-done = bf16[64,12,6144]{2,1,0:T(8,128)(2,1)} async-done(((bf16[1,12,6144]{2,1,0:T(8,128)(2,1)}), bf16[64,12,6144]{2,1,0:T(8,128)(2,1)}) %all-gather.6.cloned.1.call-update) | async-done | bytes 9437200 | tf_op jit(solution)/shard_map/all_gather | solution.py:47
  134.4 13.7 %reshape.78 = bf16[768,6144]{1,0:T(8,128)(2,1)} reshape(bf16[64,12,6144]{2,1,0:T(8,128)(2,1)} %all-gather.6.cloned.1.call-done) | data formatting | bytes 18874368
  148.2 0.0 copy-done
  148.2 0.0 copy-start.1
  148.2 0.0 copy-start.4
  148.2 6.1 %fusion.5 = f32[768,128]{1,0:T(8,128)S(1)} fusion(bf16[768,6144]{1,0:T(8,128)(2,1)} %reshape.78, bf16[1,6144,128]{2,1,0:T(8,128)(2,1)S(1)} %copy-done), kind=kOutput, calls=%fused_computation.6 | convolution fusion | flops 1207959552 | bytes 11403264 | tf_op jit(solution)/shard_map/dot_general | solution.py:48
  154.3 0.3 copy-done.1
  154.6 0.4 copy-done.4
  155.0 0.0 copy-start.3
  155.0 0.0 copy-start.2
  155.0 3.3 fusion.10
  158.3 0.0 all-gather.4.cloned.1.call-update
  158.3 0.0 copy-done.3
  158.3 124.3 %all-gather.4.cloned.1.call-done = bf16[768,8192]{1,0:T(8,128)(2,1)} async-done(((bf16[768,128]{1,0:T(8,128)(2,1)}), bf16[768,8192]{1,0:T(8,128)(2,1)}) %all-gather.4.cloned.1.call-update) | async-done | bytes 12582928 | tf_op jit(solution)/shard_map/all_gather | solution.py:51
  282.6 0.0 copy-done.2
  282.6 8.6 %fusion.13 = bf16[768,96]{0,1:T(8,128)(2,1)S(1)} fusion(bf16[768,8192]{1,0:T(8,128)(2,1)} %all-gather.4.cloned.1.call-done, bf16[1,96,8192]{2,1,0:T(8,128)(2,1)S(1)} %copy-done.2), kind=kOutput, calls=%fused_computation.10 | convolution fusion | flops 1208033280 | bytes 14303232 | tf_op jit(solution)/shard_map/dot_general | solution.py:52
  291.2 0.2 copy.21
  291.4 0.8 all_to_all.14
  292.1 7.6 %all-to-all-start = ((bf16[64,12,96]{2,1,0:T(8,128)(2,1)}), bf16[64,12,96]{2,1,0:T(8,128)(2,1)S(1)}, u32[]{:S(2)}, u32[]{:S(2)}) async-start(bf16[64,12,96]{2,1,0:T(8,128)(2,1)} %all_to_all.14), calls=%async_computation | async-start | bytes 524288 | tf_op jit(solution)/shard_map/all_to_all | solution.py:56
  299.8 0.1 copy.20
  299.9 0.1 mul.20
  300.0 0.2 fusion.17
  300.2 13.3 %all-to-all-done = bf16[64,12,96]{2,1,0:T(8,128)(2,1)S(1)} async-done(((bf16[64,12,96]{2,1,0:T(8,128)(2,1)}), bf16[64,12,96]{2,1,0:T(8,128)(2,1)S(1)}, u32[]{:S(2)}, u32[]{:S(2)}) %all-to-all-start) | async-done | bytes 147488 | tf_op jit(solution)/shard_map/all_to_all | solution.py:56
  313.5 0.1 copy.22
  313.5 0.3 all_to_all.17
  313.8 0.4 fusion.40
  314.3 1.9 collective-permute-start
  316.2 2.0 collective-permute-done
  318.1 0.1 add.22
  318.2 2.4 collective-permute-start.1
  320.6 14.9 %collective-permute-done.1 = f32[24,6144]{1,0:T(8,128)S(1)} collective-permute-done((f32[24,6144]{1,0:T(8,128)S(1)}, f32[24,6144]{1,0:T(8,128)S(1)}, u32[]{:S(2)}, u32[]{:S(2)}) %collective-permute-start.1) | collective-permute-done | bytes 589856 | tf_op jit(solution)/shard_map/ppermute | solution.py:67
  335.5 0.1 add.23
  335.5 3.9 %collective-permute-start.2 = (f32[24,6144]{1,0:T(8,128)S(1)}, f32[24,6144]{1,0:T(8,128)S(1)}, u32[]{:S(2)}, u32[]{:S(2)}) collective-permute-start(f32[24,6144]{1,0:T(8,128)S(1)} %add.23), channel_id=1, source_target_pairs={{0,256},{64,320},{128,384},{192,448},{256,0},{320,64},{384,128},{4... | collective-permute-start | bytes 1769480 | tf_op jit(solution)/shard_map/ppermute | solution.py:67
  339.4 14.0 %collective-permute-done.2 = f32[24,6144]{1,0:T(8,128)S(1)} collective-permute-done((f32[24,6144]{1,0:T(8,128)S(1)}, f32[24,6144]{1,0:T(8,128)S(1)}, u32[]{:S(2)}, u32[]{:S(2)}) %collective-permute-start.2) | collective-permute-done | bytes 589856 | tf_op jit(solution)/shard_map/ppermute | solution.py:67
  353.5 0.6 fusion.16
  (5 shorter events, 0.0 us)
Async XLA Ops:
  6.5 141.6 %copy-start = (bf16[1,6144,128]{2,1,0:T(8,128)(2,1)S(1)}, bf16[1,6144,128]{2,1,0:T(8,128)(2,1)}, u32[]{:S(2)}) copy-start(bf16[1,6144,128]{2,1,0:T(8,128)(2,1)} %param.9) | copy-start | bytes 4718596
  6.5 127.9 %all-gather.6.cloned.1.call-start = ((), (), s32[]{:S(2)}) async-start(), calls=%async_computation.2 | async-start | bytes 12779520 | tf_op jit(solution)/shard_map/all_gather | solution.py:47
  9.9 272.7 %all-gather.4.cloned.1.call-start = ((), (), s32[]{:S(2)}) async-start(), calls=%async_computation.1 | async-start | bytes 12779520 | tf_op jit(solution)/shard_map/all_gather | solution.py:51
  148.2 6.4 %copy-start.1 = (bf16[768,6144]{1,0:T(8,128)(2,1)S(1)}, bf16[768,6144]{1,0:T(8,128)(2,1)}, u32[]{:S(2)}) copy-start(bf16[768,6144]{1,0:T(8,128)(2,1)} %reshape.78) | copy-start | bytes 28311556
  148.2 6.9 %copy-start.4 = (bf16[1,6144,128]{2,1,0:T(8,128)(2,1)S(1)}, bf16[1,6144,128]{2,1,0:T(8,128)(2,1)}, u32[]{:S(2)}) copy-start(bf16[1,6144,128]{2,1,0:T(8,128)(2,1)} %param.10) | copy-start | bytes 4718596
  155.0 3.3 copy-start.3
  155.0 127.6 %copy-start.2 = (bf16[1,96,8192]{2,1,0:T(8,128)(2,1)S(1)}, bf16[1,96,8192]{2,1,0:T(8,128)(2,1)}, u32[]{:S(2)}) copy-start(bf16[1,96,8192]{2,1,0:T(8,128)(2,1)} %param.11) | copy-start | bytes 4718596
  292.1 21.3 %all-to-all-start = ((bf16[64,12,96]{2,1,0:T(8,128)(2,1)}), bf16[64,12,96]{2,1,0:T(8,128)(2,1)S(1)}, u32[]{:S(2)}, u32[]{:S(2)}) async-start(bf16[64,12,96]{2,1,0:T(8,128)(2,1)} %all_to_all.14), calls=%async_computation | async-start | bytes 524288 | tf_op jit(solution)/shard_map/all_to_all | solution.py:56
  314.3 3.9 %collective-permute-start = (f32[24,6144]{1,0:T(8,128)S(1)}, f32[24,6144]{1,0:T(8,128)S(1)}, u32[]{:S(2)}, u32[]{:S(2)}) collective-permute-start(f32[24,6144]{1,0:T(8,128)S(1)} %fusion.40), channel_id=1, source_target_pairs={{0,64},{64,0},{128,192},{192,128},{256,320},{320,256},{384,448},{4... | collective-permute-start | bytes 1769480 | tf_op jit(solution)/shard_map/ppermute | solution.py:67
  318.2 17.3 %collective-permute-start.1 = (f32[24,6144]{1,0:T(8,128)S(1)}, f32[24,6144]{1,0:T(8,128)S(1)}, u32[]{:S(2)}, u32[]{:S(2)}) collective-permute-start(f32[24,6144]{1,0:T(8,128)S(1)} %add.22), channel_id=1, source_target_pairs={{0,128},{64,192},{128,0},{192,64},{256,384},{320,448},{384,256},{4... | collective-permute-start | bytes 1769480 | tf_op jit(solution)/shard_map/ppermute | solution.py:67
  335.5 17.9 %collective-permute-start.2 = (f32[24,6144]{1,0:T(8,128)S(1)}, f32[24,6144]{1,0:T(8,128)S(1)}, u32[]{:S(2)}, u32[]{:S(2)}) collective-permute-start(f32[24,6144]{1,0:T(8,128)S(1)} %add.23), channel_id=1, source_target_pairs={{0,256},{64,320},{128,384},{192,448},{256,0},{320,64},{384,128},{4... | collective-permute-start | bytes 1769480 | tf_op jit(solution)/shard_map/ppermute | solution.py:67
Sparse Core Ops, SparseCore 0:
  10.4 123.9 all-gather.5
  158.4 124.1 all-gather.3
